TPU v7x, 32 devices: a whole 2x2x4 slice. The times are simulated.
32 devices in a mesh: pb: 8 (over z, x), row: 4 (over y, core).
Axes of the slice: x: 2, y: 2, z: 4, core: 2. Of those that a mesh axis runs over, the one named last changes fastest.
Arguments:
- kernels: bfloat16 [8, 4096, 4096], P('pb', 'row'), may hold values from -6 to 6
- orbitals: bfloat16 [4096, 1024], P('pb'), may hold values from -0.75 to 0.75
- pairs: int32 [8, 4, 2], replicated, may hold values from 0 to 15
- k_slot: int32 [16], replicated, may hold values from 0 to 15, each once
- pair_count: int32 [8], replicated, may hold values from 1 to 4, as said below
Outputs:
- exchange_fields: float32 [4, 1024, 1024], P('row', 'pb')
Inputs may be any that keep to these rules, and one draw needn't show every extreme that they name: `k_slot`: every slot holds exactly one k-point. pairs p < pair_count[q] are live; some transfer vector has all 4 live.
All inputs are finite; a program needn't handle non-finite values.
Results may differ from a plain program's by a relative error of at most 0.0029.
Values may be sent and summed in bfloat16 or wider, within the bound.
A program may use at most 128 MiB of HBM per device.

v0:
```python
import jax
import jax.numpy as jnp
from jax import lax
from jax.sharding import PartitionSpec as P


def slot_lookup(k_ids, k_slot):
    positions = jnp.arange(k_slot.shape[0], dtype=jnp.int32)
    return jnp.sum(jnp.where(k_ids[..., None] == positions, k_slot, 0), axis=-1)


def pair_products(weight, orbital_basis, pair_index, orb_width, pair_total, row_start, row_count):
    orb_left = lax.dynamic_slice_in_dim(orbital_basis, pair_index * orb_width, orb_width, 1)
    orb_right = lax.dynamic_slice_in_dim(
        orbital_basis, (pair_total + pair_index) * orb_width, orb_width, 1
    )
    left_rows = lax.dynamic_slice_in_dim(orb_left, row_start, row_count, 0)
    right_rows = lax.dynamic_slice_in_dim(orb_right, row_start, row_count, 0)
    contract = (((1,), (1,)), ((), ()))
    right_gram = lax.dot_general(
        right_rows, orb_right, contract, preferred_element_type=jnp.float32
    )
    first_term = jnp.dot(
        (weight * right_gram).astype(jnp.bfloat16), orb_left, preferred_element_type=jnp.float32
    )
    left_gram = lax.dot_general(left_rows, orb_left, contract, preferred_element_type=jnp.float32)
    second_hadamard = (weight * left_gram).astype(jnp.bfloat16)
    second_term = lax.dot_general(
        second_hadamard, right_rows, (((0,), (0,)), ((), ())), preferred_element_type=jnp.float32
    )
    return (first_term, second_term)


def shards(kernels, orbitals, pairs, k_slot, pair_count):
    pb_count = lax.axis_size("pb")
    row_devices = lax.axis_size("row")
    here_row = lax.axis_index("row")
    weight = kernels[0]
    row_count = weight.shape[0]
    point_total = weight.shape[1]
    pair_total = pairs.shape[1]
    k_total = k_slot.shape[0]
    orb_width = orbitals.shape[1] // k_total
    local_points = orbitals.shape[0]
    local_orbs = orbitals.reshape(local_points, k_total, orb_width)
    wanted = jnp.concatenate(
        [slot_lookup(pairs[:, :, 0], k_slot), slot_lookup(pairs[:, :, 1], k_slot)], axis=1
    )
    slot_share = 2 * pair_total // row_devices
    my_slots = lax.dynamic_slice_in_dim(wanted, here_row * slot_share, slot_share, 1)
    picked = jnp.take(local_orbs, my_slots, axis=1).reshape(
        local_points, pb_count, slot_share * orb_width
    )
    arrived_orbs = lax.all_to_all(picked, "pb", split_axis=1, concat_axis=0, tiled=True)
    orbital_basis = lax.all_gather(
        arrived_orbs.reshape(point_total, slot_share * orb_width), "row", axis=1, tiled=True
    )
    row_start = here_row * row_count
    first_list = []
    second_list = []
    for pair_index in range(pair_total):
        first_term, second_term = pair_products(
            weight, orbital_basis, pair_index, orb_width, pair_total, row_start, row_count
        )
        first_list.append(first_term)
        second_list.append(second_term)
    first_block = jnp.concatenate(first_list, axis=1)
    second_block = jnp.concatenate(second_list, axis=1)
    second_whole = lax.psum(second_block, "row")
    second_rows = lax.dynamic_slice_in_dim(second_whole, row_start, row_count, 0)
    contrib = jnp.concatenate([first_block, second_rows], axis=1)
    arrived = lax.all_to_all(contrib, "pb", split_axis=0, concat_axis=1, tiled=True)
    point_share = row_count // pb_count
    arrived = arrived.reshape(point_share, pb_count * 2 * pair_total, orb_width)
    targets = jnp.concatenate([pairs[:, :, 0], pairs[:, :, 1]], axis=1)
    pair_ids = jnp.arange(pair_total, dtype=jnp.int32)
    live_half = pair_ids[None, :] < pair_count[:, None]
    live_mask = jnp.concatenate([live_half, live_half], axis=1)
    k_ids = jnp.arange(k_total, dtype=jnp.int32)
    onehot = jnp.where((targets[..., None] == k_ids) & live_mask[..., None], 1.0, 0.0).astype(
        jnp.float32
    )
    onehot = onehot.reshape(pb_count * 2 * pair_total, k_total)
    fields = jnp.einsum("msn,sk->mkn", arrived, onehot, precision=lax.Precision.HIGHEST)
    return fields.reshape(1, point_share, k_total * orb_width)


def solution(mesh):
    placed = (P("pb", "row", None), P("pb", None), P(), P(), P())
    return jax.shard_map(
        shards, mesh=mesh, in_specs=placed, out_specs=P("row", "pb", None), check_vma=False
    )
```

profile of v0, /device:TPU:0, one launch (start us, length us, event | category | flops | bytes accessed | tf_op | source)
XLA Modules:
  0.0 276.9 jit_solution(14889424699236633594)
XLA Ops:
  6.5 0.0 all-gather.2.cloned.1.call-start
  6.5 0.8 fusion.76
  7.3 0.9 select_reduce_fusion.1
  8.3 0.1 copy.19
  8.4 0.1 broadcast_in_dim.45
  8.5 0.1 broadcast_in_dim.46
  8.5 0.1 copy.21
  8.6 0.1 reshape.42
  8.7 1.5 copy.20
  10.2 0.6 gather_fusion
  10.8 0.2 broadcast_select_fusion
  11.1 32.8 %all_to_all.31 = bf16[512,8,128]{0,2,1:T(8,128)(2,1)S(1)} all-to-all(bf16[512,8,128]{0,2,1:T(8,128)(2,1)S(1)} %broadcast_select_fusion), channel_id=1, replica_groups=mesh['pb'=8,'row'=4] {'pb'}, dimensions={1} | all-to-all | bytes 2097152 | tf_op jit(solution)/shard_map/all_to_all | solution.py:54
  43.9 1.3 copy.22
  45.2 0.0 all-gather.2.cloned.1.call-update
  45.2 0.0 all-reduce.2.cloned.1.call-start
  45.3 34.1 %all-gather.2.cloned.1.call-done = bf16[4096,512]{1,0:T(8,128)(2,1)} async-done(((bf16[4096,128]{1,0:T(8,128)(2,1)}), bf16[4096,512]{1,0:T(8,128)(2,1)}) %all-gather.2.cloned.1.call-update) | async-done | bytes 4194320 | tf_op jit(solution)/shard_map/all_gather | solution.py:55
  79.4 5.8 %fusion.75 = (bf16[4096,64]{1,0:T(8,128)(2,1)}, bf16[4096,64]{1,0:T(8,128)(2,1)}, bf16[4096,64]{1,0:T(8,128)(2,1)S(1)}, bf16[4096,64]{1,0:T(8,128)(2,1)}, bf16[4...) fusion(bf16[4096,512]{1,0:T(8,128)(2,1)} %all-gather.2.cloned.1.c, ...), kind=kLoop, calls=%fused_computation.82 | loop fusion | bytes 8388608 | tf_op jit(solution)/shard_map/dynamic_slice | solution.py:13
  85.2 0.0 copy-start
  85.2 0.0 copy-start.1
  85.3 9.3 %fusion.11 = f32[4096,64]{0,1:T(8,128)} fusion(bf16[4096,64]{1,0:T(8,128)(2,1)} %get-tuple-element.9, bf16[1,1024,4096]{2,1,0:T(8,128)(2,1)} %param.5, s32[]{:T(128)S(6)} %select_n.42, bf16[4096,64]{1,0:T(8,128)(2,1)} %get-tuple-element.16), kind=kOutput, calls=%fused_computation.21 | convolution fusion | flops 1086324736 | bytes 11011072 | tf_op jit(solution)/shard_map/dot_general | solution.py:28
  94.5 8.6 %fusion.8 = f32[4096,64]{0,1:T(8,128)} fusion(bf16[4096,64]{1,0:T(8,128)(2,1)} %get-tuple-element.10, bf16[1,1024,4096]{2,1,0:T(8,128)(2,1)} %param.5, s32[]{:T(128)S(6)} %select_n.42, bf16[4096,64]{1,0:T(8,128)(2,1)S(1)} %get-tuple-element.11), kind=kOutput, calls=%fused_computation.18 | convolution fusion | flops 1086324736 | bytes 11011072 | tf_op jit(solution)/shard_map/dot_general | solution.py:28
  103.1 0.0 copy-done
  103.1 8.5 %fusion.9 = f32[4096,64]{0,1:T(8,128)} fusion(bf16[4096,64]{1,0:T(8,128)(2,1)} %get-tuple-element.12, bf16[1,1024,4096]{2,1,0:T(8,128)(2,1)} %param.5, s32[]{:T(128)S(6)} %select_n.42, bf16[4096,64]{1,0:T(8,128)(2,1)S(1)} %get-tuple-element.13), kind=kOutput, calls=%fused_computation.19 | convolution fusion | flops 1086324736 | bytes 11011072 | tf_op jit(solution)/shard_map/dot_general | solution.py:28
  111.7 0.0 copy-start.2
  111.7 0.0 copy-done.1
  111.7 8.8 %fusion.10 = f32[4096,64]{0,1:T(8,128)} fusion(bf16[4096,64]{1,0:T(8,128)(2,1)} %get-tuple-element.14, bf16[1,1024,4096]{2,1,0:T(8,128)(2,1)} %param.5, s32[]{:T(128)S(6)} %select_n.42, bf16[4096,64]{1,0:T(8,128)(2,1)S(1)} %get-tuple-element.15), kind=kOutput, calls=%fused_computation.20 | convolution fusion | flops 1086324736 | bytes 11011072 | tf_op jit(solution)/shard_map/dot_general | solution.py:28
  120.5 0.0 copy-done.2
  120.5 4.3 %pad_maximum_fusion = f32[4096,256]{0,1:T(8,128)} fusion(f32[4096,64]{0,1:T(8,128)} %fusion.8, f32[4096,64]{0,1:T(8,128)} %fusion.9, f32[4096,64]{0,1:T(8,128)} %fusion.10, f32[4096,64]{0,1:T(8,128)S(1)} %copy-done.2), kind=kLoop, calls=%fused_computation.17 | loop fusion | flops 3145728 | bytes 8388608 | tf_op jit(solution)/shard_map/concatenate | solution.py:68
  124.8 0.0 all-reduce.2.cloned.1.call-update
  124.8 8.8 %fusion.21 = f32[1024,512]{0,1:T(8,128)S(1)} fusion(bf16[4096,64]{1,0:T(8,128)(2,1)} %get-tuple-element.16, bf16[1,1024,4096]{2,1,0:T(8,128)(2,1)} %param.5, s32[]{:T(128)S(6)} %select_n.42, bf16[4096,512]{1,0:T(8,128)(2,1)} %all-gather.2.cloned.1.call-done), kind=kOutput, calls=%fused_computation.30 | convolution fusion | flops 1086324736 | bytes 11010052 | tf_op jit(solution)/shard_map/dot_general | solution.py:23
  133.6 8.9 %fusion.22 = f32[1024,512]{0,1:T(8,128)S(1)} fusion(f32[1024,512]{0,1:T(8,128)S(1)} %fusion.21, bf16[4096,64]{1,0:T(8,128)(2,1)} %copy-done.1, bf16[1,1024,4096]{2,1,0:T(8,128)(2,1)} %param.5, s32[]{:T(128)S(6)} %select_n.42, bf16[4096,512]{1,0:T(8,128)(2,1)} %all-gather.2.cloned.1.call-done), kind=kOutput, calls=%fused_computation.31 | convolution fusion | flops 1086324736 | bytes 11010052 | tf_op jit(solution)/shard_map/dot_general | solution.py:23
  142.5 9.2 %fusion.23 = f32[1024,512]{0,1:T(8,128)S(1)} fusion(f32[1024,512]{0,1:T(8,128)S(1)} %fusion.22, bf16[4096,64]{1,0:T(8,128)(2,1)} %copy-done, bf16[1,1024,4096]{2,1,0:T(8,128)(2,1)} %param.5, s32[]{:T(128)S(6)} %select_n.42, bf16[4096,512]{1,0:T(8,128)(2,1)} %all-gather.2.cloned.1.call-done), kind=kOutput, calls=%fused_computation.32 | convolution fusion | flops 1086324736 | bytes 11010052 | tf_op jit(solution)/shard_map/dot_general | solution.py:23
  151.7 0.0 copy-start.3
  151.7 8.5 %fusion.24 = f32[1024,512]{0,1:T(8,128)S(1)} fusion(f32[1024,512]{0,1:T(8,128)S(1)} %fusion.23, bf16[4096,64]{1,0:T(8,128)(2,1)S(1)} %get-tuple-element.11, bf16[1,1024,4096]{2,1,0:T(8,128)(2,1)} %param.5, s32[]{:T(128)S(6)} %select_n.42, bf16[4096,512]{1,0:T(8,128)(2,1)} %all-gather.2.cloned.1.call-done), kind=kOutput, calls=%fused_computation.33 | convolution fusion | flops 1086324736 | bytes 11010052 | tf_op jit(solution)/shard_map/dot_general | solution.py:23
  160.2 50.3 %all-reduce.2.cloned.1.call-done = f32[4096,256]{0,1:T(8,128)} async-done(((f32[4096,256]{0,1:T(8,128)}), f32[4096,256]{0,1:T(8,128)}) %all-reduce.2.cloned.1.call-update) | async-done | bytes 4194320 | tf_op jit(solution)/shard_map/psum | solution.py:69
  210.5 1.3 dynamic-slice_dynamic-update-slice_fusion
  211.8 1.5 copy_bitcast_fusion
  213.3 5.5 %all-to-all-start.1 = ((f32[8,128,512]{1,2,0:T(8,128)}), f32[8,128,512]{1,2,0:T(8,128)S(1)}, u32[]{:S(2)}, u32[]{:S(2)}) async-start(f32[8,128,512]{1,2,0:T(8,128)} %copy_bitcast_fusion), calls=%async_computation.1 | async-start | bytes 4194304 | tf_op jit(solution)/shard_map/all_to_all | solution.py:72
  218.8 0.0 copy-done.3
  218.8 0.1 iota_compare_fusion.3
  218.8 0.1 pad_add_fusion.2
  218.9 0.1 and.17
  219.0 0.1 copy.18
  219.1 0.1 eq.42
  219.2 47.5 %all-to-all-done.1 = f32[8,128,512]{1,2,0:T(8,128)S(1)} async-done(((f32[8,128,512]{1,2,0:T(8,128)}), f32[8,128,512]{1,2,0:T(8,128)S(1)}, u32[]{:S(2)}, u32[]{:S(2)}) %all-to-all-start.1) | async-done | bytes 2097184 | tf_op jit(solution)/shard_map/all_to_all | solution.py:72
  266.7 2.2 fusion.18
  268.9 0.2 copy.25
  269.1 1.0 copy.26
  (4 shorter events, 0.0 us)
Async XLA Ops:
  6.5 72.9 %all-gather.2.cloned.1.call-start = ((), (), s32[]{:S(2)}) async-start(), calls=%async_computation.2 | async-start | bytes 5242880 | tf_op jit(solution)/shard_map/all_gather | solution.py:55
  45.2 165.2 %all-reduce.2.cloned.1.call-start = ((), (), s32[]{:S(2)}) async-start(), calls=%async_computation.3 | async-start | bytes 8388608 | tf_op jit(solution)/shard_map/psum | solution.py:69
  85.2 17.9 %copy-start = (bf16[4096,64]{1,0:T(8,128)(2,1)}, bf16[4096,64]{1,0:T(8,128)(2,1)S(1)}, u32[]{:S(2)}) copy-start(bf16[4096,64]{1,0:T(8,128)(2,1)S(1)} %get-tuple-element.13) | copy-start | bytes 1572868
  85.2 26.4 %copy-start.1 = (bf16[4096,64]{1,0:T(8,128)(2,1)}, bf16[4096,64]{1,0:T(8,128)(2,1)S(1)}, u32[]{:S(2)}) copy-start(bf16[4096,64]{1,0:T(8,128)(2,1)S(1)} %get-tuple-element.15) | copy-start | bytes 1572868
  111.7 8.8 %copy-start.2 = (f32[4096,64]{0,1:T(8,128)S(1)}, f32[4096,64]{0,1:T(8,128)}, u32[]{:S(2)}) copy-start(f32[4096,64]{0,1:T(8,128)} %fusion.11) | copy-start | bytes 3145732
  151.7 67.1 %copy-start.3 = (s32[8]{0:T(128)S(1)}, s32[8]{0:T(128)}, u32[]{:S(2)}) copy-start(s32[8]{0:T(128)} %param.9) | copy-start | bytes 100
  213.3 53.4 %all-to-all-start.1 = ((f32[8,128,512]{1,2,0:T(8,128)}), f32[8,128,512]{1,2,0:T(8,128)S(1)}, u32[]{:S(2)}, u32[]{:S(2)}) async-start(f32[8,128,512]{1,2,0:T(8,128)} %copy_bitcast_fusion), calls=%async_computation.1 | async-start | bytes 4194304 | tf_op jit(solution)/shard_map/all_to_all | solution.py:72
Sparse Core Ops, SparseCore 0:
  45.3 34.0 all-gather.1
  124.9 85.4 all-reduce.1
where the time goes:
time: 277 us
  waiting for transfers between devices  132 us (48%)
  matrix products  72.9 us (26%)
  blocking collectives  32.8 us (12%)
  local copies, waits for them, and re-layouts  14.6 us (5%)
  between operations  13.5 us (5%)
  other arithmetic  5.63 us (2%)
  starting transfers between devices  5.55 us (2%)
    psum x1, waiting for transfers between devices, shards(): second_whole = lax.psum(second_block, 'row')  50.3 us
    all_to_all x1, waiting for transfers between devices, shards(): lax.all_to_all(contrib, 'pb', split_axis=0, concat_axis=1, tiled=True)  47.5 us
    dot_general x4, matrix products, pair_products(): jnp.dot((weight * right_gram).astype(jnp.bfloat16), orb_left, preferred_e...  35.4 us
    dot_general x4, matrix products, pair_products(): lax.dot_general(second_hadamard, right_rows, (((0,), (0,)), ((), ())), pr...  35.2 us
    all_gather x1, waiting for transfers between devices, shards(): lax.all_gather(arrived_orbs.reshape(point_total, slot_share * orb_width),...  34.1 us
    all_to_all x1, blocking collectives, shards(): lax.all_to_all(picked, 'pb', split_axis=1, concat_axis=0, tiled=True)  32.8 us
    dynamic_slice x1, local copies, waits for them, and re-layouts, pair_products(): lax.dynamic_slice_in_dim(orbital_basis, pair_index * orb_width, orb_width...  5.82 us
  transfers between devices with their start and end apart: 3, of which 3 were waited for; matrix products, arithmetic and copies ran while one was open for 13% of the time, Pallas kernels for 0%

commit v1 on v0

--- a/solution.py
+++ b/solution.py
@@ -2,6 +2,28 @@
 import jax.numpy as jnp
 from jax import lax
 from jax.sharding import PartitionSpec as P
+
+
+def in_order(parts, dim):
+    parts = jnp.moveaxis(parts, 0, dim)
+    dims = parts.shape
+    return parts.reshape(*dims[:dim], dims[dim] * dims[dim + 1], *dims[dim + 2 :])
+
+
+def doubled(x, axis):
+    peers = lax.axis_size(axis)
+    tiles = x[None]
+    for level in range(peers.bit_length() - 1):
+        stride = 1 << level
+        other = lax.ppermute(tiles, axis, [(i, i ^ stride) for i in range(peers)])
+        both = jnp.stack([tiles, other])
+        upper = lax.axis_index(axis) >> level & 1
+        tiles = jnp.where(upper == 0, both, both[::-1]).reshape(-1, *x.shape)
+    return tiles
+
+
+def collect(shard, axis, dim):
+    return in_order(doubled(shard, axis), dim)
 
 
 def slot_lookup(k_ids, k_slot):
@@ -52,9 +74,7 @@
         local_points, pb_count, slot_share * orb_width
     )
     arrived_orbs = lax.all_to_all(picked, "pb", split_axis=1, concat_axis=0, tiled=True)
-    orbital_basis = lax.all_gather(
-        arrived_orbs.reshape(point_total, slot_share * orb_width), "row", axis=1, tiled=True
-    )
+    orbital_basis = collect(arrived_orbs.reshape(point_total, slot_share * orb_width), "row", 1)
     row_start = here_row * row_count
     first_list = []
     second_list = []

time: 277 us -> 299 us (1.079)
  waiting for transfers between devices: 132 us -> 146 us
  matrix products: 72.9 us -> 66.9 us
  other arithmetic: 5.63 us -> 11.6 us
  local copies, waits for them, and re-layouts: 14.6 us -> 19.3 us
    ppermute x0 -> x2, waiting for transfers between devices: none -> 49.1 us  [doubled(): other = lax.ppermute(tiles, axis, [(i, i ^ stride) for i in range(peers)])]
    all_gather x1 -> x0, waiting for transfers between devices: 34.1 us -> none  [shards(): lax.all_gather(arrived_orbs.reshape(point_total, slot_share * orb_width),...]
    reshape x0 -> x1, local copies, waits for them, and re-layouts: none -> 6.46 us  [doubled(): tiles = jnp.where(upper == 0, both, both[::-1]).reshape(-1, *x.shape)]
    dot_general x4, matrix products: 35.2 us -> 31 us  [pair_products(): lax.dot_general(second_hadamard, right_rows, (((0,), (0,)), ((), ())), pr...]
    another operation x0 -> x3, other arithmetic: none -> 4.05 us  [doubled(): both = jnp.stack([tiles, other])]
  transfers between devices with their start and end apart: 3 -> 4, of which waited for: 3 -> 4; matrix products, arithmetic and copies ran while one was open for 13% -> 11% of each run, Pallas kernels for 0% -> 0%
where the time goes in v1:
time: 299 us; the launch traced here: 298 us
  waiting for transfers between devices  146 us (49%)
  matrix products  66.9 us (22%)
  blocking collectives  32.8 us (11%)
  local copies, waits for them, and re-layouts  19.3 us (6%)
  between operations  13.6 us (5%)
  other arithmetic  11.6 us (4%)
  starting transfers between devices  7.1 us (2%)
    psum x1, waiting for transfers between devices, shards(): second_whole = lax.psum(second_block, 'row')  49.8 us
    ppermute x2, waiting for transfers between devices, doubled(): other = lax.ppermute(tiles, axis, [(i, i ^ stride) for i in range(peers)])  49.1 us
    all_to_all x1, waiting for transfers between devices, shards(): lax.all_to_all(contrib, 'pb', split_axis=0, concat_axis=1, tiled=True)  47.5 us
    dot_general x4, matrix products, pair_products(): jnp.dot((weight * right_gram).astype(jnp.bfloat16), orb_left, preferred_e...  33.7 us
    all_to_all x1, blocking collectives, shards(): lax.all_to_all(picked, 'pb', split_axis=1, concat_axis=0, tiled=True)  32.8 us
    dot_general x4, matrix products, pair_products(): lax.dot_general(second_hadamard, right_rows, (((0,), (0,)), ((), ())), pr...  31 us
    reshape x1, local copies, waits for them, and re-layouts, doubled(): tiles = jnp.where(upper == 0, both, both[::-1]).reshape(-1, *x.shape)  6.46 us
  transfers between devices with their start and end apart: 4, of which 4 were waited for; matrix products, arithmetic and copies ran while one was open for 11% of the time, Pallas kernels for 0%

profile of v1, /device:TPU:0, one launch (start us, length us, event | category | flops | bytes accessed | tf_op | source)
XLA Modules:
  0.0 297.9 jit_solution(9298992009451815168)
XLA Ops:
  6.5 0.0 all-reduce.2.cloned.1.call-start
  6.5 1.5 copy.22
  8.0 0.8 fusion.78
  8.8 0.9 select_reduce_fusion.1
  9.8 0.1 copy.23
  9.9 0.1 reshape.51
  10.0 0.1 copy.21
  10.1 0.1 broadcast_in_dim.45
  10.1 0.1 broadcast_in_dim.46
  10.2 0.6 gather_fusion
  10.8 0.2 broadcast_select_fusion
  11.1 32.8 %all_to_all.31 = bf16[512,8,128]{0,2,1:T(8,128)(2,1)S(1)} all-to-all(bf16[512,8,128]{0,2,1:T(8,128)(2,1)S(1)} %broadcast_select_fusion), channel_id=1, replica_groups=mesh['pb'=8,'row'=4] {'pb'}, dimensions={1} | all-to-all | bytes 2097152 | tf_op jit(solution)/shard_map/all_to_all | solution.py:76
  43.9 0.7 copy.24
  44.6 0.1 collective-permute-start
  44.6 2.6 collective-permute-done
  47.3 0.2 pad_maximum_fusion.2
  47.5 1.9 fusion.19
  49.4 1.5 collective-permute-start.1
  50.9 46.5 %collective-permute-done.1 = bf16[2,4096,128]{2,1,0:T(8,128)(2,1)} collective-permute-done((bf16[2,4096,128]{2,1,0:T(8,128)(2,1)}, bf16[2,4096,128]{2,1,0:T(8,128)(2,1)}, u32[]{:S(2)}, u32[]{:S(2)}) %collective-permute-start.1) | collective-permute-done | bytes 2097184 | tf_op jit(solution)/shard_map/ppermute | solution.py:18
  97.4 2.0 pad_maximum_fusion
  99.3 2.8 reverse_select_fusion
  102.1 6.5 %copy.26 = bf16[4,4096,128]{1,2,0:T(8,128)(2,1)} copy(bf16[4,4096,128]{2,1,0:T(8,128)(2,1)} %bitcast.84) | data formatting | bytes 8388608 | tf_op jit(solution)/shard_map/reshape | solution.py:21
  108.6 3.7 %fusion.77 = (bf16[4096,64]{0,1:T(8,128)(2,1)}, bf16[4096,64]{0,1:T(8,128)(2,1)S(1)}, bf16[4096,64]{0,1:T(8,128)(2,1)S(1)}, bf16[4096,64]{0,1:T(8,128)(2,1)S(1)}...) fusion(bf16[4096,512]{0,1:T(8,128)(2,1)} %bitcast.79), kind=kLoop, calls=%fused_computation.88 | loop fusion | bytes 8388608 | tf_op jit(solution)/shard_map/dynamic_slice | solution.py:35
  112.2 7.5 %fusion.8 = f32[4096,64]{0,1:T(8,128)S(1)} fusion(bf16[4096,64]{0,1:T(8,128)(2,1)S(1)} %get-tuple-element.10, bf16[1,1024,4096]{2,1,0:T(8,128)(2,1)} %param.5, s32[]{:T(128)S(6)} %select_n.62, bf16[4096,64]{0,1:T(8,128)(2,1)S(1)} %get-tuple-element.11), kind=kOutput, calls=%fused_computation.21 | convolution fusion | flops 1086324736 | bytes 10224640 | tf_op jit(solution)/shard_map/dot_general | solution.py:50
  119.8 7.2 %fusion.9 = f32[4096,64]{0,1:T(8,128)S(1)} fusion(bf16[4096,64]{0,1:T(8,128)(2,1)S(1)} %get-tuple-element.12, bf16[1,1024,4096]{2,1,0:T(8,128)(2,1)} %param.5, s32[]{:T(128)S(6)} %select_n.62, bf16[4096,64]{0,1:T(8,128)(2,1)S(1)} %get-tuple-element.13), kind=kOutput, calls=%fused_computation.22 | convolution fusion | flops 1086324736 | bytes 10224640 | tf_op jit(solution)/shard_map/dot_general | solution.py:50
  127.0 7.5 %fusion.10 = f32[4096,64]{0,1:T(8,128)S(1)} fusion(bf16[4096,64]{0,1:T(8,128)(2,1)} %get-tuple-element.14, bf16[1,1024,4096]{2,1,0:T(8,128)(2,1)} %param.5, s32[]{:T(128)S(6)} %select_n.62, bf16[4096,64]{0,1:T(8,128)(2,1)} %get-tuple-element.15), kind=kOutput, calls=%fused_computation.23 | convolution fusion | flops 1086324736 | bytes 10224640 | tf_op jit(solution)/shard_map/dot_general | solution.py:50
  134.5 8.8 %fusion.11 = f32[4096,64]{0,1:T(8,128)} fusion(bf16[4096,64]{0,1:T(8,128)(2,1)} %get-tuple-element.9, bf16[1,1024,4096]{2,1,0:T(8,128)(2,1)} %param.5, s32[]{:T(128)S(6)} %select_n.62, bf16[4096,64]{0,1:T(8,128)(2,1)} %get-tuple-element.16), kind=kOutput, calls=%fused_computation.24 | convolution fusion | flops 1086324736 | bytes 10224640 | tf_op jit(solution)/shard_map/dot_general | solution.py:50
  143.3 3.5 %pad_maximum_fusion.1 = f32[4096,256]{0,1:T(8,128)} fusion(f32[4096,64]{0,1:T(8,128)S(1)} %fusion.8, f32[4096,64]{0,1:T(8,128)S(1)} %fusion.9, f32[4096,64]{0,1:T(8,128)S(1)} %fusion.10, f32[4096,64]{0,1:T(8,128)} %fusion.11), kind=kLoop, calls=%fused_computation.19 | loop fusion | flops 3145728 | bytes 8388608 | tf_op jit(solution)/shard_map/concatenate | solution.py:88
  146.7 0.0 all-reduce.2.cloned.1.call-update
  146.8 1.0 copy-done.5
  147.8 8.4 %fusion.23 = f32[1024,512]{0,1:T(8,128)S(1)} fusion(bf16[4096,64]{0,1:T(8,128)(2,1)S(1)} %copy-done.5, bf16[1,1024,4096]{2,1,0:T(8,128)(2,1)} %param.5, s32[]{:T(128)S(6)} %select_n.62, bf16[4096,512]{0,1:T(8,128)(2,1)} %bitcast.80), kind=kOutput, calls=%fused_computation.36 | convolution fusion | flops 1086324736 | bytes 9830404 | tf_op jit(solution)/shard_map/dot_general | solution.py:45
  156.2 8.4 %fusion.24 = f32[1024,512]{0,1:T(8,128)S(1)} fusion(f32[1024,512]{0,1:T(8,128)S(1)} %fusion.23, bf16[4096,64]{0,1:T(8,128)(2,1)S(1)} %copy-done.4, bf16[1,1024,4096]{2,1,0:T(8,128)(2,1)} %param.5, s32[]{:T(128)S(6)} %select_n.62, bf16[4096,512]{0,1:T(8,128)(2,1)} %bitcast.81), kind=kOutput, calls=%fused_computation.37 | convolution fusion | flops 1086324736 | bytes 9830404 | tf_op jit(solution)/shard_map/dot_general | solution.py:45
  164.6 8.4 %fusion.25 = f32[1024,512]{0,1:T(8,128)S(1)} fusion(f32[1024,512]{0,1:T(8,128)S(1)} %fusion.24, bf16[4096,64]{0,1:T(8,128)(2,1)S(1)} %copy-done.3, bf16[1,1024,4096]{2,1,0:T(8,128)(2,1)} %param.5, s32[]{:T(128)S(6)} %select_n.62, bf16[4096,512]{0,1:T(8,128)(2,1)} %bitcast.82), kind=kOutput, calls=%fused_computation.38 | convolution fusion | flops 1086324736 | bytes 9830404 | tf_op jit(solution)/shard_map/dot_general | solution.py:45
  173.0 8.6 %fusion.26 = f32[1024,512]{0,1:T(8,128)S(1)} fusion(f32[1024,512]{0,1:T(8,128)S(1)} %fusion.25, bf16[4096,64]{0,1:T(8,128)(2,1)S(1)} %copy-done.1, bf16[1,1024,4096]{2,1,0:T(8,128)(2,1)} %param.5, s32[]{:T(128)S(6)} %select_n.62, bf16[4096,512]{0,1:T(8,128)(2,1)} %bitcast.83), kind=kOutput, calls=%fused_computation.39 | convolution fusion | flops 1086324736 | bytes 9830404 | tf_op jit(solution)/shard_map/dot_general | solution.py:45
  181.6 49.8 %all-reduce.2.cloned.1.call-done = f32[4096,256]{0,1:T(8,128)} async-done(((f32[4096,256]{0,1:T(8,128)}), f32[4096,256]{0,1:T(8,128)}) %all-reduce.2.cloned.1.call-update) | async-done | bytes 4194320 | tf_op jit(solution)/shard_map/psum | solution.py:89
  231.4 1.3 dynamic-slice_dynamic-update-slice_fusion
  232.7 0.0 copy-start.6
  232.8 1.5 copy_bitcast_fusion
  234.2 5.5 %all-to-all-start.1 = ((f32[8,128,512]{1,2,0:T(8,128)}), f32[8,128,512]{1,2,0:T(8,128)S(1)}, u32[]{:S(2)}, u32[]{:S(2)}) async-start(f32[8,128,512]{1,2,0:T(8,128)} %copy_bitcast_fusion), calls=%async_computation.1 | async-start | bytes 4194304 | tf_op jit(solution)/shard_map/all_to_all | solution.py:92
  239.7 0.1 copy.20
  239.8 0.1 eq.48
  239.9 0.1 iota_compare_fusion.3
  240.0 0.1 pad_add_fusion.2
  240.1 0.1 and.23
  240.1 47.5 %all-to-all-done.1 = f32[8,128,512]{1,2,0:T(8,128)S(1)} async-done(((f32[8,128,512]{1,2,0:T(8,128)}), f32[8,128,512]{1,2,0:T(8,128)S(1)}, u32[]{:S(2)}, u32[]{:S(2)}) %all-to-all-start.1) | async-done | bytes 2097184 | tf_op jit(solution)/shard_map/all_to_all | solution.py:92
  287.7 2.2 fusion.20
  289.9 0.2 copy.29
  290.1 1.0 copy.30
  (16 shorter events, 0.1 us)
Async XLA Ops:
  6.5 224.9 %all-reduce.2.cloned.1.call-start = ((), (), s32[]{:S(2)}) async-start(), calls=%async_computation.2 | async-start | bytes 8388608 | tf_op jit(solution)/shard_map/psum | solution.py:89
  44.6 2.7 collective-permute-start
  49.4 48.0 %collective-permute-start.1 = (bf16[2,4096,128]{2,1,0:T(8,128)(2,1)}, bf16[2,4096,128]{2,1,0:T(8,128)(2,1)}, u32[]{:S(2)}, u32[]{:S(2)}) collective-permute-start(bf16[2,4096,128]{2,1,0:T(8,128)(2,1)} %get-tuple-element.18), channel_id=1, source_target_pairs={{0,2},{1,3},{2,0},{3,1},{4,6},{5,7},{6,4},{7,5},{8,10},{9,11},{10,... | collective-permute-start | bytes 6291464 | tf_op jit(solution)/shard_map/ppermute | solution.py:18
  112.2 7.6 %copy-start = (bf16[4096,64]{0,1:T(8,128)(2,1)}, bf16[4096,64]{0,1:T(8,128)(2,1)S(1)}, u32[]{:S(2)}) copy-start(bf16[4096,64]{0,1:T(8,128)(2,1)S(1)} %get-tuple-element.11) | copy-start | bytes 1572868
  112.2 7.6 %copy-start.2 = (bf16[4096,64]{0,1:T(8,128)(2,1)}, bf16[4096,64]{0,1:T(8,128)(2,1)S(1)}, u32[]{:S(2)}) copy-start(bf16[4096,64]{0,1:T(8,128)(2,1)S(1)} %get-tuple-element.13) | copy-start | bytes 1572868
  146.7 1.0 copy-start.5
  147.8 8.4 %copy-start.4 = (bf16[4096,64]{0,1:T(8,128)(2,1)S(1)}, bf16[4096,64]{0,1:T(8,128)(2,1)}, u32[]{:S(2)}) copy-start(bf16[4096,64]{0,1:T(8,128)(2,1)} %get-tuple-element.15) | copy-start | bytes 1572868
  156.2 8.4 %copy-start.3 = (bf16[4096,64]{0,1:T(8,128)(2,1)S(1)}, bf16[4096,64]{0,1:T(8,128)(2,1)}, u32[]{:S(2)}) copy-start(bf16[4096,64]{0,1:T(8,128)(2,1)} %copy-done.2) | copy-start | bytes 1572868
  164.6 8.4 %copy-start.1 = (bf16[4096,64]{0,1:T(8,128)(2,1)S(1)}, bf16[4096,64]{0,1:T(8,128)(2,1)}, u32[]{:S(2)}) copy-start(bf16[4096,64]{0,1:T(8,128)(2,1)} %copy-done) | copy-start | bytes 1572868
  232.7 7.2 %copy-start.6 = (s32[8]{0:T(128)S(1)}, s32[8]{0:T(128)}, u32[]{:S(2)}) copy-start(s32[8]{0:T(128)} %param.9) | copy-start | bytes 100
  234.2 53.4 %all-to-all-start.1 = ((f32[8,128,512]{1,2,0:T(8,128)}), f32[8,128,512]{1,2,0:T(8,128)S(1)}, u32[]{:S(2)}, u32[]{:S(2)}) async-start(f32[8,128,512]{1,2,0:T(8,128)} %copy_bitcast_fusion), calls=%async_computation.1 | async-start | bytes 4194304 | tf_op jit(solution)/shard_map/all_to_all | solution.py:92
Sparse Core Ops, SparseCore 0:
  146.9 84.5 all-reduce.1
